TPU v7x, 32 devices: a whole 2x2x4 slice. The times are simulated.
32 devices in a mesh: atom: 16 (over z, x, core), energy: 2 (over y).
Axes of the slice: x: 2, y: 2, z: 4, core: 2. Of those that a mesh axis runs over, the one named last changes fastest.
Arguments:
- single_site: float32 [256, 2, 2, 1024], P('atom', 'energy'), may hold values from -2 to 2
- structure: float32 [2, 26, 2, 1024], P('energy'), may hold values from -0.4375 to 0.4375
- neighbours: int32 [256, 26], P('atom'), may hold values from 0 to 255, as said below
- species: int32 [256], P('atom'), may hold values from 0 to 1
- valence: float32 [2], replicated, may hold values from 0.5 to 3
- energy_weights: float32 [2, 2], P('energy'), may hold values from -4 to 4
- gaunt_table: float32 [49, 1024], replicated, may hold values from -1.5 to 1.5
- radial_shapes: float32 [2, 2, 2, 49, 512], P(None, 'energy'), may hold values from -6 to 6
- radial_weights: float32 [512], replicated, may hold values from 0.001 to 0.03
- madelung: float32 [256, 256], P('atom'), may hold values from -0.375 to 0.375
- old_potential: float32 [256, 49, 512], P('atom', None, 'energy'), may hold values from -6 to 6
Outputs:
- density: float32 [256, 49, 512], P('atom', None, 'energy')
- potential: float32 [256, 49, 512], P('atom', None, 'energy')
Inputs may be any that keep to these rules, and one draw needn't show every extreme that they name: `neighbours`: atom a lies in lattice plane a // 16; the 16 planes close periodically. Slots 0 to 8 name distinct atoms of the plane before a's, slots 9 to 16 distinct atoms of a's own plane other than a, slots 17 to 25 distinct atoms of the plane after. Direction 26 - 1 - k is the reverse of direction k; this only says which structure constants pair up, and the neighbour lists need not be reciprocal.
All inputs are finite; a program needn't handle non-finite values.
Results may differ from a plain program's by a relative error of at most 0.0001.
Values sent between devices are 32-bit elements; how exact they have to be, the bound alone decides.
A program may use at most 64 MiB of HBM per device.

v0:
```python
import jax
import jax.numpy as jnp
from jax import lax
from jax.sharding import PartitionSpec as P

ORDER = 32
DIRS = 26
PLANE = 16
TERMS = 4
SPECIES = 2
mixing = 0.3
highest = lax.Precision.HIGHEST


def with_halo(block, sides, width):
    for axis, dim in sides:
        count = lax.axis_size(axis)
        forward = [(i, i + 1) for i in range(count - 1)]
        forward.append((count - 1, 0))
        backward = [(target, source) for source, target in forward]
        low = lax.ppermute(
            lax.slice_in_dim(block, block.shape[dim] - width, None, axis=dim), axis, forward
        )
        high = lax.ppermute(lax.slice_in_dim(block, 0, width, axis=dim), axis, backward)
        block = jnp.concatenate([low, block, high], axis=dim)
    return block


def matmul_high(former, latter):
    return jnp.matmul(former, latter, precision=highest)


def complex_product(former, latter):
    former_real = former[..., 0, :, :]
    former_imag = former[..., 1, :, :]
    latter_real = latter[..., 0, :, :]
    latter_imag = latter[..., 1, :, :]
    real_part = matmul_high(former_real, latter_real) - matmul_high(former_imag, latter_imag)
    imag_part = matmul_high(former_real, latter_imag) + matmul_high(former_imag, latter_real)
    return jnp.stack([real_part, imag_part], axis=-3)


def shards(
    single_site,
    structure,
    neighbours,
    species,
    valence,
    energy_weights,
    gaunt_table,
    radial_shapes,
    radial_weights,
    madelung,
    old_potential,
):
    atom_rows = single_site.shape[0]
    energy_rows = single_site.shape[1]
    extended = with_halo(single_site, (("atom", 0),), PLANE)
    extended = extended.reshape(extended.shape[0], energy_rows, 2, ORDER, ORDER)
    site_matrices = single_site.reshape(atom_rows, energy_rows, 2, ORDER, ORDER)
    couplings = structure.reshape(energy_rows, DIRS, 2, ORDER, ORDER)
    first_atom = lax.axis_index("atom") * atom_rows
    total_atoms = lax.axis_size("atom") * atom_rows
    local_rows = (neighbours - first_atom + PLANE) % total_atoms
    group_size = DIRS // 2
    forward_all = jnp.moveaxis(couplings, 1, 0)
    backward_all = forward_all[::-1]
    forward_groups = forward_all.reshape(2, group_size, energy_rows, 2, ORDER, ORDER)
    backward_groups = backward_all.reshape(2, group_size, energy_rows, 2, ORDER, ORDER)
    row_groups = jnp.transpose(local_rows).reshape(2, group_size, atom_rows)

    def add_group(accumulated, inputs):
        forward, backward, rows = inputs
        gathered = jnp.take(extended, rows, axis=0)
        left = complex_product(forward[:, None], gathered)
        terms = complex_product(left, backward[:, None])
        return (accumulated + jnp.sum(terms, axis=0), None)

    coupled, _ = lax.scan(
        add_group, jnp.zeros_like(site_matrices), (forward_groups, backward_groups, row_groups)
    )
    propagator = complex_product(site_matrices, coupled)
    series_term = site_matrices
    path_operator = site_matrices
    for power in range(TERMS - 1):
        series_term = complex_product(propagator, series_term)
        path_operator = path_operator + series_term
    flat = path_operator.reshape(atom_rows, energy_rows, 2, ORDER * ORDER)
    projected = jnp.einsum("aezq,lq->aezl", flat, gaunt_table, precision=highest)
    weight_real = energy_weights[:, 0][None, :, None]
    weight_imag = energy_weights[:, 1][None, :, None]
    scaled_real = weight_real * projected[:, :, 0] - weight_imag * projected[:, :, 1]
    scaled_imag = weight_real * projected[:, :, 1] + weight_imag * projected[:, :, 0]
    slice_width = old_potential.shape[2]
    energy_index = lax.axis_index("energy")
    kinds = jnp.arange(SPECIES, dtype=jnp.int32)
    one_hot = jnp.where(species[:, None] == kinds[None, :], jnp.float32(1.0), jnp.float32(0.0))
    valence_of = jnp.sum(one_hot * valence[None, :], axis=1)
    pieces = lax.all_to_all(radial_shapes, "energy", split_axis=4, concat_axis=1, tiled=True)
    all_real, all_imag = (
        lax.all_gather(scaled_real, "energy", axis=1, tiled=True),
        lax.all_gather(scaled_imag, "energy", axis=1, tiled=True),
    )
    sorted_real = one_hot[:, :, None, None] * all_real[:, None]
    sorted_imag = one_hot[:, :, None, None] * all_imag[:, None]
    density = jnp.einsum("asel,selr->alr", sorted_real, pieces[:, :, 1], precision=highest)
    density = density + jnp.einsum(
        "asel,selr->alr", sorted_imag, pieces[:, :, 0], precision=highest
    )
    piece_weights = lax.dynamic_slice_in_dim(
        radial_weights, energy_index * slice_width, slice_width
    )
    partial_charge = jnp.dot(density[:, 0, :], piece_weights, precision=highest)
    local_charge = lax.psum(partial_charge, "energy") - valence_of
    charges = lax.all_gather(local_charge, "atom", axis=0, tiled=True)
    madelung_shift = jnp.dot(madelung, charges, precision=highest)
    channel = jnp.arange(density.shape[1], dtype=jnp.int32)[None, :, None]
    added = jnp.where(channel == 0, madelung_shift[:, None, None], jnp.float32(0.0))
    potential = (1.0 - mixing) * old_potential + mixing * (density + added)
    return (density, potential)


def solution(mesh):
    in_specs = (
        P("atom", "energy", None, None),
        P("energy", None, None, None),
        P("atom", None),
        P("atom"),
        P(),
        P("energy", None),
        P(),
        P(None, "energy", None, None, None),
        P(),
        P("atom", None),
        P("atom", None, "energy"),
    )
    out_specs = (P("atom", None, "energy"), P("atom", None, "energy"))
    return jax.shard_map(shards, mesh=mesh, in_specs=in_specs, out_specs=out_specs, check_vma=False)
```

profile of v0, /device:TPU:0, one launch (start us, length us, event | category | flops | bytes accessed | tf_op | source)
XLA Modules:
  0.0 190.3 jit_solution(6027028950451602410)
XLA Ops:
  1.2 5.0 %collective-permute-start.1 = (f32[16,1,2,1024]{3,2,1,0:T(2,128)}, f32[16,1,2,1024]{3,2,1,0:T(2,128)S(1)}, u32[]{:S(2)}, u32[]{:S(2)}) collective-permute-start(f32[16,1,2,1024]{3,2,1,0:T(2,128)} %param.13), channel_id=1, source_target_pairs={{2,0},{4,2},{6,4},{8,6},{10,8},{12,10},{14,12},{16,14},{18,16},{20... | collective-permute-start | bytes 393224 | tf_op jit(solution)/shard_map/ppermute | solution.py:24
  10.4 4.2 %all-to-all-start = ((f32[2,1,50176]{2,1,0:T(1,128)}), f32[2,1,50176]{2,1,0:T(1,128)}, u32[]{:S(2)}, u32[]{:S(2)}) async-start(f32[2,1,50176]{2,1,0:T(1,128)} %reshape.313), calls=%async_computation | async-start | bytes 802816 | tf_op jit(solution)/shard_map/all_to_all | solution.py:99
  23.6 100.0 %while.11 = (s32[]{:T(128)}, f32[16,1,2,32,32]{4,3,0,2,1:T(8,128)S(1)}, f32[2,13,1,2,32,32]{5,4,3,1,0,2:T(8,128)}, s32[2,13,16]{1,0,2:T(2,128)S(1)}, f32[48,1,2,...) while((s32[]{:T(128)}, ...), condition=%wide.region_2.3_spmd.clone, body=%wide.region_0.2_spmd.clone.sunk | while | flops 656476992 | bytes 64435708 | solution.py:79
  42.8 3.9 %gather_fusion = f32[208,2,32,32]{3,2,1,0:T(8,128)} fusion(f32[48,2,32,32]{3,2,1,0:T(8,128)S(1)} %bitcast.229, s32[1024]{0:T(1024)S(1)} %pad_clamp_fusion.2), kind=kCustom, calls=%fused_computation.clone.clone.1 | custom fusion | bytes 3408704 | tf_op jit(solution)/shard_map/while/body/eval_jaxpr/jit(_take)/gather | solution.py:74
  46.6 3.7 %copy.172 = f32[208,2,32,32]{3,2,0,1:T(8,128)S(1)} copy(f32[208,2,32,32]{3,2,1,0:T(8,128)} %gather_fusion) | data formatting | bytes 3407872 | tf_op jit(solution)/shard_map/while/body/eval_jaxpr/jit(_take)/gather | solution.py:74
  55.1 3.3 %fusion.82 = f32[13,32,16,32]{3,1,2,0:T(8,128)S(1)} fusion(f32[13,32,16,32]{3,1,2,0:T(8,128)S(1)} %fusion.81, f32[13,16,1,2,32,32]{5,4,1,0,3,2:T(8,128)S(1)} %broadcast_select_fusion.3, f32[13,1,1,2,32,32]{5,4,0,3,2,1:T(8,128)S(1)} %bitcast.236), kind=kOutput, calls=%fused_computation.19.clone.1 | convolution fusion | flops 82001920 | bytes 7880704 | tf_op jit(solution)/shard_map/while/body/eval_jaxpr/dot_general | solution.py:30
  58.4 3.2 %fusion.78 = f32[13,32,16,32]{3,1,2,0:T(8,128)S(1)} fusion(f32[13,16,1,2,32,32]{5,4,1,0,3,2:T(8,128)S(1)} %broadcast_select_fusion.3, f32[13,1,1,2,32,32]{5,4,0,3,2,1:T(8,128)S(1)} %bitcast.237), kind=kOutput, calls=%fused_computation.15.clone.1 | convolution fusion | flops 81788928 | bytes 4472832 | tf_op jit(solution)/shard_map/while/body/eval_jaxpr/dot_general | solution.py:30
  61.6 3.3 %fusion.79 = f32[13,32,16,32]{3,1,2,0:T(8,128)S(1)} fusion(f32[13,32,16,32]{3,1,2,0:T(8,128)S(1)} %fusion.78, f32[13,16,1,2,32,32]{5,4,1,0,3,2:T(8,128)S(1)} %broadcast_select_fusion.3, f32[13,1,1,2,32,32]{5,4,0,3,2,1:T(8,128)S(1)} %bitcast.238), kind=kOutput, calls=%fused_computation.20.clone.1 | convolution fusion | flops 82001920 | bytes 7880704 | tf_op jit(solution)/shard_map/while/body/eval_jaxpr/dot_general | solution.py:30
  64.9 3.3 %fusion.83 = f32[13,16,32,32]{3,2,1,0:T(8,128)S(1)} fusion(f32[13,32,16,32]{3,1,2,0:T(8,128)S(1)} %fusion.79, f32[13,1,1,2,32,32]{5,4,0,3,2,1:T(8,128)S(1)} %bitcast.231), kind=kOutput, calls=%fused_computation.6.clone.1 | convolution fusion | flops 81788928 | bytes 4472832 | tf_op jit(solution)/shard_map/while/body/eval_jaxpr/dot_general | solution.py:30
  68.2 3.4 %subtract_bitcast_fusion.2 = f32[13,16,1,1,32,32]{5,4,1,0,3,2:T(8,128)S(1)} fusion(f32[13,16,32,32]{3,2,1,0:T(8,128)S(1)} %fusion.83, f32[13,32,16,32]{3,1,2,0:T(8,128)S(1)} %fusion.82, f32[13,1,1,2,32,32]{5,4,0,3,2,1:T(8,128)S(1)} %bitcast.232), kind=kOutput, calls=%fused_computation.13.clone.1 | convolution fusion | flops 82001920 | bytes 7880704 | tf_op jit(solution)/shard_map/while/body/eval_jaxpr/dot_general | solution.py:30
  71.6 3.3 %fusion.80 = f32[13,16,32,32]{3,2,1,0:T(8,128)S(1)} fusion(f32[13,32,16,32]{3,1,2,0:T(8,128)S(1)} %fusion.79, f32[13,1,1,2,32,32]{5,4,0,3,2,1:T(8,128)S(1)} %bitcast.233), kind=kOutput, calls=%fused_computation.4.clone.1 | convolution fusion | flops 81788928 | bytes 4472832 | tf_op jit(solution)/shard_map/while/body/eval_jaxpr/dot_general | solution.py:30
  74.9 3.4 %add_bitcast_fusion.2 = f32[13,16,1,1,32,32]{5,4,1,0,3,2:T(8,128)S(1)} fusion(f32[13,16,32,32]{3,2,1,0:T(8,128)S(1)} %fusion.80, f32[13,32,16,32]{3,1,2,0:T(8,128)S(1)} %fusion.82, f32[13,1,1,2,32,32]{5,4,0,3,2,1:T(8,128)S(1)} %bitcast.234), kind=kOutput, calls=%fused_computation.12.clone.1 | convolution fusion | flops 82001920 | bytes 7880704 | tf_op jit(solution)/shard_map/while/body/eval_jaxpr/dot_general | solution.py:30
  79.5 3.9 %gather_fusion = f32[208,2,32,32]{3,2,1,0:T(8,128)} fusion(f32[48,2,32,32]{3,2,1,0:T(8,128)S(1)} %bitcast.229, s32[1024]{0:T(1024)S(1)} %pad_clamp_fusion.2), kind=kCustom, calls=%fused_computation.clone.clone.1 | custom fusion | bytes 3408704 | tf_op jit(solution)/shard_map/while/body/eval_jaxpr/jit(_take)/gather | solution.py:74
  83.4 3.7 %copy.172 = f32[208,2,32,32]{3,2,0,1:T(8,128)S(1)} copy(f32[208,2,32,32]{3,2,1,0:T(8,128)} %gather_fusion) | data formatting | bytes 3407872 | tf_op jit(solution)/shard_map/while/body/eval_jaxpr/jit(_take)/gather | solution.py:74
  91.9 3.3 %fusion.82 = f32[13,32,16,32]{3,1,2,0:T(8,128)S(1)} fusion(f32[13,32,16,32]{3,1,2,0:T(8,128)S(1)} %fusion.81, f32[13,16,1,2,32,32]{5,4,1,0,3,2:T(8,128)S(1)} %broadcast_select_fusion.3, f32[13,1,1,2,32,32]{5,4,0,3,2,1:T(8,128)S(1)} %bitcast.236), kind=kOutput, calls=%fused_computation.19.clone.1 | convolution fusion | flops 82001920 | bytes 7880704 | tf_op jit(solution)/shard_map/while/body/eval_jaxpr/dot_general | solution.py:30
  98.4 3.3 %fusion.79 = f32[13,32,16,32]{3,1,2,0:T(8,128)S(1)} fusion(f32[13,32,16,32]{3,1,2,0:T(8,128)S(1)} %fusion.78, f32[13,16,1,2,32,32]{5,4,1,0,3,2:T(8,128)S(1)} %broadcast_select_fusion.3, f32[13,1,1,2,32,32]{5,4,0,3,2,1:T(8,128)S(1)} %bitcast.238), kind=kOutput, calls=%fused_computation.20.clone.1 | convolution fusion | flops 82001920 | bytes 7880704 | tf_op jit(solution)/shard_map/while/body/eval_jaxpr/dot_general | solution.py:30
  101.7 3.3 %fusion.83 = f32[13,16,32,32]{3,2,1,0:T(8,128)S(1)} fusion(f32[13,32,16,32]{3,1,2,0:T(8,128)S(1)} %fusion.79, f32[13,1,1,2,32,32]{5,4,0,3,2,1:T(8,128)S(1)} %bitcast.231), kind=kOutput, calls=%fused_computation.6.clone.1 | convolution fusion | flops 81788928 | bytes 4472832 | tf_op jit(solution)/shard_map/while/body/eval_jaxpr/dot_general | solution.py:30
  105.0 3.4 %subtract_bitcast_fusion.2 = f32[13,16,1,1,32,32]{5,4,1,0,3,2:T(8,128)S(1)} fusion(f32[13,16,32,32]{3,2,1,0:T(8,128)S(1)} %fusion.83, f32[13,32,16,32]{3,1,2,0:T(8,128)S(1)} %fusion.82, f32[13,1,1,2,32,32]{5,4,0,3,2,1:T(8,128)S(1)} %bitcast.232), kind=kOutput, calls=%fused_computation.13.clone.1 | convolution fusion | flops 82001920 | bytes 7880704 | tf_op jit(solution)/shard_map/while/body/eval_jaxpr/dot_general | solution.py:30
  108.3 3.3 %fusion.80 = f32[13,16,32,32]{3,2,1,0:T(8,128)S(1)} fusion(f32[13,32,16,32]{3,1,2,0:T(8,128)S(1)} %fusion.79, f32[13,1,1,2,32,32]{5,4,0,3,2,1:T(8,128)S(1)} %bitcast.233), kind=kOutput, calls=%fused_computation.4.clone.1 | convolution fusion | flops 81788928 | bytes 4472832 | tf_op jit(solution)/shard_map/while/body/eval_jaxpr/dot_general | solution.py:30
  111.6 3.4 %add_bitcast_fusion.2 = f32[13,16,1,1,32,32]{5,4,1,0,3,2:T(8,128)S(1)} fusion(f32[13,16,32,32]{3,2,1,0:T(8,128)S(1)} %fusion.80, f32[13,32,16,32]{3,1,2,0:T(8,128)S(1)} %fusion.82, f32[13,1,1,2,32,32]{5,4,0,3,2,1:T(8,128)S(1)} %bitcast.234), kind=kOutput, calls=%fused_computation.12.clone.1 | convolution fusion | flops 82001920 | bytes 7880704 | tf_op jit(solution)/shard_map/while/body/eval_jaxpr/dot_general | solution.py:30
  136.2 4.4 %all-gather.1 = f32[16,2,1,49]{3,0,2,1:T(8,128)S(1)} all-gather(f32[16,1,1,49]{3,0,2,1:T(8,128)S(1)} %get-tuple-element.89), channel_id=3, replica_groups=mesh['atom'=16,'energy'=2] {'energy'}, dimensions={1}, use_global_device_ids=true | all-gather | bytes 9408 | tf_op jit(solution)/shard_map/all_gather | solution.py:102
  140.6 4.6 %all-gather = f32[16,2,1,49]{3,0,2,1:T(8,128)S(1)} all-gather(f32[16,1,1,49]{3,0,2,1:T(8,128)S(1)} %get-tuple-element.88), channel_id=2, replica_groups=mesh['atom'=16,'energy'=2] {'energy'}, dimensions={1}, use_global_device_ids=true | all-gather | bytes 9408 | tf_op jit(solution)/shard_map/all_gather | solution.py:101
  153.1 4.9 %psum.7 = f32[16]{0:T(128)S(1)} all-reduce(f32[16]{0:T(128)S(1)} %convolution_bitcast_fusion.4), channel_id=1, replica_groups=mesh['atom'=16,'energy'=2] {'energy'}, use_global_device_ids=true, to_apply=%region_3.4 | all-reduce | flops 16 | bytes 128 | tf_op jit(solution)/shard_map/psum | solution.py:114
  158.1 29.5 %all-reduce = f32[256]{0:T(256)S(1)} all-reduce(f32[256]{0:T(256)S(1)} %subtract_dynamic-update-slice_fusion), channel_id=1, replica_groups=mesh['atom'=16,'energy'=2] {'atom'}, use_global_device_ids=true, to_apply=%add | all-reduce | flops 256 | bytes 2048
  (130 shorter events, 50.9 us)
Async XLA Ops:
  0.6 134.0 %copy-start = (f32[49,1024]{1,0:T(8,128)S(1)}, f32[49,1024]{1,0:T(8,128)}, u32[]{:S(2)}) copy-start(f32[49,1024]{1,0:T(8,128)} %param.19) | copy-start | bytes 602116
  0.6 15.7 %copy-start.5 = (f32[16,1,2,1024]{3,2,1,0:T(2,128)S(1)}, f32[16,1,2,1024]{3,2,1,0:T(2,128)}, u32[]{:S(2)}) copy-start(f32[16,1,2,1024]{3,2,1,0:T(2,128)} %param.13) | copy-start | bytes 393220
  0.7 13.9 %copy-start.10 = (s32[16,26]{1,0:T(8,128)S(1)}, s32[16,26]{1,0:T(8,128)}, u32[]{:S(2)}) copy-start(s32[16,26]{1,0:T(8,128)} %param.15) | copy-start | bytes 4996
  0.7 14.0 %copy-start.15 = (s32[16]{0:T(128)S(1)}, s32[16]{0:T(128)}, u32[]{:S(2)}) copy-start(s32[16]{0:T(128)} %param.16) | copy-start | bytes 196
  0.7 14.0 %copy-start.14 = (f32[2]{0:T(128)S(1)}, f32[2]{0:T(128)}, u32[]{:S(2)}) copy-start(f32[2]{0:T(128)} %param.17) | copy-start | bytes 28
  0.7 15.7 %copy-start.7 = (f32[1,26,2,1024]{3,2,1,0:T(2,128)S(1)}, f32[1,26,2,1024]{3,2,1,0:T(2,128)}, u32[]{:S(2)}) copy-start(f32[1,26,2,1024]{3,2,1,0:T(2,128)} %param.14) | copy-start | bytes 638980
  0.7 22.0 %collective-permute-start = (f32[16,1,2,1024]{3,2,1,0:T(2,128)}, f32[16,1,2,1024]{3,2,1,0:T(2,128)S(1)}, u32[]{:S(2)}, u32[]{:S(2)}) collective-permute-start(f32[16,1,2,1024]{3,2,1,0:T(2,128)} %param.13), channel_id=1, source_target_pairs={{0,2},{2,4},{4,6},{6,8},{8,10},{10,12},{12,14},{14,16},{16,18},{18... | collective-permute-start | bytes 393224 | tf_op jit(solution)/shard_map/ppermute | solution.py:21
  1.2 21.5 %collective-permute-start.1 = (f32[16,1,2,1024]{3,2,1,0:T(2,128)}, f32[16,1,2,1024]{3,2,1,0:T(2,128)S(1)}, u32[]{:S(2)}, u32[]{:S(2)}) collective-permute-start(f32[16,1,2,1024]{3,2,1,0:T(2,128)} %param.13), channel_id=1, source_target_pairs={{2,0},{4,2},{6,4},{8,6},{10,8},{12,10},{14,12},{16,14},{18,16},{20... | collective-permute-start | bytes 393224 | tf_op jit(solution)/shard_map/ppermute | solution.py:24
  7.9 12.3 %copy-start.16 = (f32[512]{0:T(512)S(1)}, f32[512]{0:T(512)}, u32[]{:S(2)}) copy-start(f32[512]{0:T(512)} %param.21) | copy-start | bytes 6148
  7.9 12.9 %copy-start.18 = (u32[32]{0:T(128)S(1)}, u32[32]{0:T(128)}, u32[]{:S(2)}) copy-start(u32[32]{0:T(128)} %constant.72) | copy-start | bytes 388
  7.9 14.2 %copy-start.12 = (f32[1,2]{1,0:T(1,128)S(1)}, f32[1,2]{1,0:T(1,128)}, u32[]{:S(2)}) copy-start(f32[1,2]{1,0:T(1,128)} %param.18) | copy-start | bytes 28
  10.4 134.9 %all-to-all-start = ((f32[2,1,50176]{2,1,0:T(1,128)}), f32[2,1,50176]{2,1,0:T(1,128)}, u32[]{:S(2)}, u32[]{:S(2)}) async-start(f32[2,1,50176]{2,1,0:T(1,128)} %reshape.313), calls=%async_computation | async-start | bytes 802816 | tf_op jit(solution)/shard_map/all_to_all | solution.py:99
  23.6 100.3 %copy-start.1 = (f32[16,1,2,32,32]{4,3,0,2,1:T(8,128)S(1)}, f32[16,1,2,32,32]{4,3,0,2,1:T(8,128)}, u32[]{:S(2)}) copy-start(f32[16,1,2,32,32]{4,3,0,2,1:T(8,128)} %reshape.276) | copy-start | bytes 393220
  50.4 1.2 copy-start.2
  50.4 1.4 copy-start.3
  87.1 1.2 copy-start.2
  87.1 1.4 copy-start.3
  130.3 4.0 %copy-start.6 = (f32[16,1,2,1024]{3,2,1,0:T(2,128)S(1)}, f32[16,1,2,1024]{3,2,1,0:T(2,128)}, u32[]{:S(2)}) copy-start(f32[16,1,2,1024]{3,2,1,0:T(2,128)} %param.13) | copy-start | bytes 393220
  133.4 17.7 %copy-start.9 = (f32[16,2]{0,1:T(2,128)S(1)}, f32[16,2]{0,1:T(2,128)}, u32[]{:S(2)}) copy-start(f32[16,2]{0,1:T(2,128)} %get-tuple-element.91) | copy-start | bytes 388
  136.1 16.8 %copy-start.11 = (f32[256]{0:T(256)S(1)}, f32[256]{0:T(256)}, u32[]{:S(2)}) copy-start(f32[256]{0:T(256)} %dynamic_slice.14) | copy-start | bytes 3076
  140.5 17.5 %copy-start.13 = (f32[16]{0:T(128)S(1)}, f32[16]{0:T(128)}, u32[]{:S(2)}) copy-start(f32[16]{0:T(128)} %get-tuple-element.90) | copy-start | bytes 196
  140.5 47.1 %copy-start.8 = (f32[16,256]{1,0:T(8,128)S(1)}, f32[16,256]{1,0:T(8,128)}, u32[]{:S(2)}) copy-start(f32[16,256]{1,0:T(8,128)} %param.22) | copy-start | bytes 49156
  140.5 47.2 %copy-start.17 = (pred[49]{0:T(512)(128)(4,1)S(1)}, pred[49]{0:T(512)(128)(4,1)}, u32[]{:S(2)}) copy-start(pred[49]{0:T(512)(128)(4,1)} %iota_compare_fusion) | copy-start | bytes 151
  153.0 37.1 %copy-start.4 = (f32[16,49,256]{2,0,1:T(8,128)}, f32[16,49,256]{2,0,1:T(8,128)S(1)}, u32[]{:S(2)}) copy-start(f32[16,49,256]{2,0,1:T(8,128)S(1)} %fusion.19) | copy-start | bytes 2408452
where the time goes:
time: 194 us; the launch traced here: 190 us
  matrix products  64.2 us (33%)
  blocking collectives  43.3 us (22%)
  local copies, waits for them, and re-layouts  32.3 us (17%)
  loops' own time  26.8 us (14%)
  other arithmetic  11.9 us (6%)
  starting transfers between devices  9.73 us (5%)
  between operations  2.05 us (1%)
    dot_general x32, matrix products, matmul_high(): return jnp.matmul(former, latter, precision=highest)  61.7 us
    unnamed x1, blocking collectives  29.5 us
    another operation x1, loops' own time, shards(): lax.scan(add_group, jnp.zeros_like(site_matrices), (forward_groups, backw...  26.8 us
    gather x4, local copies, waits for them, and re-layouts, add_group(): gathered = jnp.take(extended, rows, axis=0)  15.2 us
    unnamed x40, local copies, waits for them, and re-layouts  6.71 us
    ppermute x1, starting transfers between devices, with_halo(): lax.ppermute(lax.slice_in_dim(block, 0, width, axis=dim), axis, backward)  5.02 us
    psum x1, blocking collectives, shards(): local_charge = lax.psum(partial_charge, 'energy') - valence_of  4.92 us
    all_gather x1, blocking collectives, shards(): lax.all_gather(scaled_real, 'energy', axis=1, tiled=True)  4.56 us
  transfers between devices with their start and end apart: 3, of which 0 were waited for; matrix products, arithmetic and copies ran while one was open for 51% of the time, Pallas kernels for 0%

commit v1 on v0

--- a/solution.py
+++ b/solution.py
@@ -10,6 +10,13 @@
 SPECIES = 2
 mixing = 0.3
 highest = lax.Precision.HIGHEST
+
+
+def chunk_raise(here_x):
+    formed = lax.all_to_all(
+        jnp.stack(jnp.split(here_x, lax.axis_size("energy"), axis=4), axis=0), "energy", 0, 0
+    )
+    return jnp.concatenate(formed, axis=1)
 
 
 def with_halo(block, sides, width):
@@ -96,7 +103,7 @@
     kinds = jnp.arange(SPECIES, dtype=jnp.int32)
     one_hot = jnp.where(species[:, None] == kinds[None, :], jnp.float32(1.0), jnp.float32(0.0))
     valence_of = jnp.sum(one_hot * valence[None, :], axis=1)
-    pieces = lax.all_to_all(radial_shapes, "energy", split_axis=4, concat_axis=1, tiled=True)
+    pieces = chunk_raise(radial_shapes)
     all_real, all_imag = (
         lax.all_gather(scaled_real, "energy", axis=1, tiled=True),
         lax.all_gather(scaled_imag, "energy", axis=1, tiled=True),

time: 194 us -> 188 us (0.969)
  local copies, waits for them, and re-layouts: 32.3 us -> 28.6 us
    unnamed x40 -> x33, local copies, waits for them, and re-layouts: 6.71 us -> 1.64 us
    all_to_all x1 -> x0, other arithmetic: 2.81 us -> none  [shards(): lax.all_to_all(radial_shapes, 'energy', split_axis=4, concat_axis=1, tile...]
  transfers between devices with their start and end apart: 3 -> 3, of which waited for: 0 -> 0; matrix products, arithmetic and copies ran while one was open for 51% -> 52% of each run, Pallas kernels for 0% -> 0%
where the time goes in v1:
time: 188 us; the launch traced here: 185 us
  matrix products  64.1 us (34%)
  blocking collectives  43.3 us (23%)
  local copies, waits for them, and re-layouts  28.6 us (15%)
  loops' own time  26.8 us (14%)
  other arithmetic  10.3 us (5%)
  starting transfers between devices  9.73 us (5%)
  between operations  1.96 us (1%)
    dot_general x32, matrix products, matmul_high(): return jnp.matmul(former, latter, precision=highest)  61.7 us
    unnamed x1, blocking collectives  29.5 us
    another operation x1, loops' own time, shards(): lax.scan(add_group, jnp.zeros_like(site_matrices), (forward_groups, backw...  26.8 us
    gather x4, local copies, waits for them, and re-layouts, add_group(): gathered = jnp.take(extended, rows, axis=0)  15.2 us
    ppermute x1, starting transfers between devices, with_halo(): lax.ppermute(lax.slice_in_dim(block, 0, width, axis=dim), axis, backward)  5.02 us
    psum x1, blocking collectives, shards(): local_charge = lax.psum(partial_charge, 'energy') - valence_of  4.92 us
    all_gather x1, blocking collectives, shards(): lax.all_gather(scaled_real, 'energy', axis=1, tiled=True)  4.56 us
    all_gather x1, blocking collectives, shards(): lax.all_gather(scaled_imag, 'energy', axis=1, tiled=True)  4.36 us
  transfers between devices with their start and end apart: 3, of which 0 were waited for; matrix products, arithmetic and copies ran while one was open for 52% of the time, Pallas kernels for 0%

profile of v1, /device:TPU:0, one launch (start us, length us, event | category | flops | bytes accessed | tf_op | source)
XLA Modules:
  0.0 184.9 jit_solution(8031446700648571190)
XLA Ops:
  1.2 5.0 %collective-permute-start.1 = (f32[16,1,2,1024]{3,2,1,0:T(2,128)}, f32[16,1,2,1024]{3,2,1,0:T(2,128)S(1)}, u32[]{:S(2)}, u32[]{:S(2)}) collective-permute-start(f32[16,1,2,1024]{3,2,1,0:T(2,128)} %param.13), channel_id=1, source_target_pairs={{2,0},{4,2},{6,4},{8,6},{10,8},{12,10},{14,12},{16,14},{18,16},{20... | collective-permute-start | bytes 393224 | tf_op jit(solution)/shard_map/ppermute | solution.py:31
  8.6 4.2 %all-to-all-start = ((f32[2,2,1,2,49,256]{5,1,4,3,2,0:T(2,128)}), f32[2,2,1,2,49,256]{5,1,4,3,2,0:T(2,128)}, u32[]{:S(2)}, u32[]{:S(2)}) async-start(f32[2,2,1,2,49,256]{5,1,4,3,2,0:T(2,128)} %pad_maximum_fusion), calls=%async_computation | async-start | bytes 802816 | tf_op jit(solution)/shard_map/all_to_all | solution.py:16
  23.8 100.1 %while.11 = (s32[]{:T(128)}, f32[16,1,2,32,32]{4,3,0,2,1:T(8,128)S(1)}, f32[2,13,1,2,32,32]{5,4,3,1,0,2:T(8,128)}, s32[2,13,16]{1,0,2:T(2,128)S(1)}, f32[48,1,2,...) while((s32[]{:T(128)}, ...), condition=%wide.region_2.3_spmd.clone, body=%wide.region_0.2_spmd.clone.sunk | while | flops 656476992 | bytes 64435708 | solution.py:86
  43.0 3.9 %gather_fusion = f32[208,2,32,32]{3,2,1,0:T(8,128)} fusion(f32[48,2,32,32]{3,2,1,0:T(8,128)S(1)} %bitcast.232, s32[1024]{0:T(1024)S(1)} %pad_clamp_fusion.2), kind=kCustom, calls=%fused_computation.clone.clone.1 | custom fusion | bytes 3408704 | tf_op jit(solution)/shard_map/while/body/eval_jaxpr/jit(_take)/gather | solution.py:81
  46.8 3.7 %copy.146 = f32[208,2,32,32]{3,2,0,1:T(8,128)S(1)} copy(f32[208,2,32,32]{3,2,1,0:T(8,128)} %gather_fusion) | data formatting | bytes 3407872 | tf_op jit(solution)/shard_map/while/body/eval_jaxpr/jit(_take)/gather | solution.py:81
  52.1 3.2 %fusion.82 = f32[13,32,16,32]{3,1,2,0:T(8,128)S(1)} fusion(f32[13,16,1,2,32,32]{5,4,1,0,3,2:T(8,128)S(1)} %broadcast_select_fusion.3, f32[13,1,1,2,32,32]{5,4,0,3,2,1:T(8,128)S(1)} %bitcast.238), kind=kOutput, calls=%fused_computation.16.clone.1 | convolution fusion | flops 81788928 | bytes 4472832 | tf_op jit(solution)/shard_map/while/body/eval_jaxpr/dot_general | solution.py:37
  55.3 3.3 %fusion.83 = f32[13,32,16,32]{3,1,2,0:T(8,128)S(1)} fusion(f32[13,32,16,32]{3,1,2,0:T(8,128)S(1)} %fusion.82, f32[13,16,1,2,32,32]{5,4,1,0,3,2:T(8,128)S(1)} %broadcast_select_fusion.3, f32[13,1,1,2,32,32]{5,4,0,3,2,1:T(8,128)S(1)} %bitcast.239), kind=kOutput, calls=%fused_computation.19.clone.1 | convolution fusion | flops 82001920 | bytes 7880704 | tf_op jit(solution)/shard_map/while/body/eval_jaxpr/dot_general | solution.py:37
  61.8 3.3 %fusion.80 = f32[13,32,16,32]{3,1,2,0:T(8,128)S(1)} fusion(f32[13,32,16,32]{3,1,2,0:T(8,128)S(1)} %fusion.79, f32[13,16,1,2,32,32]{5,4,1,0,3,2:T(8,128)S(1)} %broadcast_select_fusion.3, f32[13,1,1,2,32,32]{5,4,0,3,2,1:T(8,128)S(1)} %bitcast.241), kind=kOutput, calls=%fused_computation.20.clone.1 | convolution fusion | flops 82001920 | bytes 7880704 | tf_op jit(solution)/shard_map/while/body/eval_jaxpr/dot_general | solution.py:37
  65.2 3.3 %fusion.84 = f32[13,16,32,32]{3,2,1,0:T(8,128)S(1)} fusion(f32[13,32,16,32]{3,1,2,0:T(8,128)S(1)} %fusion.80, f32[13,1,1,2,32,32]{5,4,0,3,2,1:T(8,128)S(1)} %bitcast.234), kind=kOutput, calls=%fused_computation.6.clone.1 | convolution fusion | flops 81788928 | bytes 4472832 | tf_op jit(solution)/shard_map/while/body/eval_jaxpr/dot_general | solution.py:37
  68.4 3.4 %subtract_bitcast_fusion.2 = f32[13,16,1,1,32,32]{5,4,1,0,3,2:T(8,128)S(1)} fusion(f32[13,16,32,32]{3,2,1,0:T(8,128)S(1)} %fusion.84, f32[13,32,16,32]{3,1,2,0:T(8,128)S(1)} %fusion.83, f32[13,1,1,2,32,32]{5,4,0,3,2,1:T(8,128)S(1)} %bitcast.235), kind=kOutput, calls=%fused_computation.13.clone.1 | convolution fusion | flops 82001920 | bytes 7880704 | tf_op jit(solution)/shard_map/while/body/eval_jaxpr/dot_general | solution.py:37
  71.8 3.3 %fusion.81 = f32[13,16,32,32]{3,2,1,0:T(8,128)S(1)} fusion(f32[13,32,16,32]{3,1,2,0:T(8,128)S(1)} %fusion.80, f32[13,1,1,2,32,32]{5,4,0,3,2,1:T(8,128)S(1)} %bitcast.236), kind=kOutput, calls=%fused_computation.4.clone.1 | convolution fusion | flops 81788928 | bytes 4472832 | tf_op jit(solution)/shard_map/while/body/eval_jaxpr/dot_general | solution.py:37
  75.1 3.4 %add_bitcast_fusion.2 = f32[13,16,1,1,32,32]{5,4,1,0,3,2:T(8,128)S(1)} fusion(f32[13,16,32,32]{3,2,1,0:T(8,128)S(1)} %fusion.81, f32[13,32,16,32]{3,1,2,0:T(8,128)S(1)} %fusion.83, f32[13,1,1,2,32,32]{5,4,0,3,2,1:T(8,128)S(1)} %bitcast.237), kind=kOutput, calls=%fused_computation.12.clone.1 | convolution fusion | flops 82001920 | bytes 7880704 | tf_op jit(solution)/shard_map/while/body/eval_jaxpr/dot_general | solution.py:37
  79.8 3.9 %gather_fusion = f32[208,2,32,32]{3,2,1,0:T(8,128)} fusion(f32[48,2,32,32]{3,2,1,0:T(8,128)S(1)} %bitcast.232, s32[1024]{0:T(1024)S(1)} %pad_clamp_fusion.2), kind=kCustom, calls=%fused_computation.clone.clone.1 | custom fusion | bytes 3408704 | tf_op jit(solution)/shard_map/while/body/eval_jaxpr/jit(_take)/gather | solution.py:81
  83.6 3.7 %copy.146 = f32[208,2,32,32]{3,2,0,1:T(8,128)S(1)} copy(f32[208,2,32,32]{3,2,1,0:T(8,128)} %gather_fusion) | data formatting | bytes 3407872 | tf_op jit(solution)/shard_map/while/body/eval_jaxpr/jit(_take)/gather | solution.py:81
  92.1 3.3 %fusion.83 = f32[13,32,16,32]{3,1,2,0:T(8,128)S(1)} fusion(f32[13,32,16,32]{3,1,2,0:T(8,128)S(1)} %fusion.82, f32[13,16,1,2,32,32]{5,4,1,0,3,2:T(8,128)S(1)} %broadcast_select_fusion.3, f32[13,1,1,2,32,32]{5,4,0,3,2,1:T(8,128)S(1)} %bitcast.239), kind=kOutput, calls=%fused_computation.19.clone.1 | convolution fusion | flops 82001920 | bytes 7880704 | tf_op jit(solution)/shard_map/while/body/eval_jaxpr/dot_general | solution.py:37
  98.6 3.3 %fusion.80 = f32[13,32,16,32]{3,1,2,0:T(8,128)S(1)} fusion(f32[13,32,16,32]{3,1,2,0:T(8,128)S(1)} %fusion.79, f32[13,16,1,2,32,32]{5,4,1,0,3,2:T(8,128)S(1)} %broadcast_select_fusion.3, f32[13,1,1,2,32,32]{5,4,0,3,2,1:T(8,128)S(1)} %bitcast.241), kind=kOutput, calls=%fused_computation.20.clone.1 | convolution fusion | flops 82001920 | bytes 7880704 | tf_op jit(solution)/shard_map/while/body/eval_jaxpr/dot_general | solution.py:37
  101.9 3.3 %fusion.84 = f32[13,16,32,32]{3,2,1,0:T(8,128)S(1)} fusion(f32[13,32,16,32]{3,1,2,0:T(8,128)S(1)} %fusion.80, f32[13,1,1,2,32,32]{5,4,0,3,2,1:T(8,128)S(1)} %bitcast.234), kind=kOutput, calls=%fused_computation.6.clone.1 | convolution fusion | flops 81788928 | bytes 4472832 | tf_op jit(solution)/shard_map/while/body/eval_jaxpr/dot_general | solution.py:37
  105.2 3.4 %subtract_bitcast_fusion.2 = f32[13,16,1,1,32,32]{5,4,1,0,3,2:T(8,128)S(1)} fusion(f32[13,16,32,32]{3,2,1,0:T(8,128)S(1)} %fusion.84, f32[13,32,16,32]{3,1,2,0:T(8,128)S(1)} %fusion.83, f32[13,1,1,2,32,32]{5,4,0,3,2,1:T(8,128)S(1)} %bitcast.235), kind=kOutput, calls=%fused_computation.13.clone.1 | convolution fusion | flops 82001920 | bytes 7880704 | tf_op jit(solution)/shard_map/while/body/eval_jaxpr/dot_general | solution.py:37
  108.6 3.3 %fusion.81 = f32[13,16,32,32]{3,2,1,0:T(8,128)S(1)} fusion(f32[13,32,16,32]{3,1,2,0:T(8,128)S(1)} %fusion.80, f32[13,1,1,2,32,32]{5,4,0,3,2,1:T(8,128)S(1)} %bitcast.236), kind=kOutput, calls=%fused_computation.4.clone.1 | convolution fusion | flops 81788928 | bytes 4472832 | tf_op jit(solution)/shard_map/while/body/eval_jaxpr/dot_general | solution.py:37
  111.9 3.4 %add_bitcast_fusion.2 = f32[13,16,1,1,32,32]{5,4,1,0,3,2:T(8,128)S(1)} fusion(f32[13,16,32,32]{3,2,1,0:T(8,128)S(1)} %fusion.81, f32[13,32,16,32]{3,1,2,0:T(8,128)S(1)} %fusion.83, f32[13,1,1,2,32,32]{5,4,0,3,2,1:T(8,128)S(1)} %bitcast.237), kind=kOutput, calls=%fused_computation.12.clone.1 | convolution fusion | flops 82001920 | bytes 7880704 | tf_op jit(solution)/shard_map/while/body/eval_jaxpr/dot_general | solution.py:37
  136.6 4.4 %all-gather.1 = f32[16,2,1,49]{3,0,2,1:T(8,128)S(1)} all-gather(f32[16,1,1,49]{3,0,2,1:T(8,128)S(1)} %get-tuple-element.85), channel_id=3, replica_groups=mesh['atom'=16,'energy'=2] {'energy'}, dimensions={1}, use_global_device_ids=true | all-gather | bytes 9408 | tf_op jit(solution)/shard_map/all_gather | solution.py:109
  141.1 4.6 %all-gather = f32[16,2,1,49]{3,0,2,1:T(8,128)S(1)} all-gather(f32[16,1,1,49]{3,0,2,1:T(8,128)S(1)} %get-tuple-element.84), channel_id=2, replica_groups=mesh['atom'=16,'energy'=2] {'energy'}, dimensions={1}, use_global_device_ids=true | all-gather | bytes 9408 | tf_op jit(solution)/shard_map/all_gather | solution.py:108
  148.9 4.9 %psum.7 = f32[16]{0:T(128)S(1)} all-reduce(f32[16]{0:T(128)S(1)} %convolution_bitcast_fusion.4), channel_id=1, replica_groups=mesh['atom'=16,'energy'=2] {'energy'}, use_global_device_ids=true, to_apply=%region_3.4 | all-reduce | flops 16 | bytes 128 | tf_op jit(solution)/shard_map/psum | solution.py:121
  153.9 29.5 %all-reduce = f32[256]{0:T(256)S(1)} all-reduce(f32[256]{0:T(256)S(1)} %subtract_dynamic-update-slice_fusion), channel_id=1, replica_groups=mesh['atom'=16,'energy'=2] {'atom'}, use_global_device_ids=true, to_apply=%add | all-reduce | flops 256 | bytes 2048
  (124 shorter events, 45.6 us)
Async XLA Ops:
  0.6 134.3 %copy-start = (f32[49,1024]{1,0:T(8,128)S(1)}, f32[49,1024]{1,0:T(8,128)}, u32[]{:S(2)}) copy-start(f32[49,1024]{1,0:T(8,128)} %param.19) | copy-start | bytes 602116
  0.6 16.1 %copy-start.7 = (f32[1,26,2,1024]{3,2,1,0:T(2,128)S(1)}, f32[1,26,2,1024]{3,2,1,0:T(2,128)}, u32[]{:S(2)}) copy-start(f32[1,26,2,1024]{3,2,1,0:T(2,128)} %param.14) | copy-start | bytes 638980
  0.7 22.3 %collective-permute-start = (f32[16,1,2,1024]{3,2,1,0:T(2,128)}, f32[16,1,2,1024]{3,2,1,0:T(2,128)S(1)}, u32[]{:S(2)}, u32[]{:S(2)}) collective-permute-start(f32[16,1,2,1024]{3,2,1,0:T(2,128)} %param.13), channel_id=1, source_target_pairs={{0,2},{2,4},{4,6},{6,8},{8,10},{10,12},{12,14},{14,16},{16,18},{18... | collective-permute-start | bytes 393224 | tf_op jit(solution)/shard_map/ppermute | solution.py:28
  1.2 21.7 %collective-permute-start.1 = (f32[16,1,2,1024]{3,2,1,0:T(2,128)}, f32[16,1,2,1024]{3,2,1,0:T(2,128)S(1)}, u32[]{:S(2)}, u32[]{:S(2)}) collective-permute-start(f32[16,1,2,1024]{3,2,1,0:T(2,128)} %param.13), channel_id=1, source_target_pairs={{2,0},{4,2},{6,4},{8,6},{10,8},{12,10},{14,12},{16,14},{18,16},{20... | collective-permute-start | bytes 393224 | tf_op jit(solution)/shard_map/ppermute | solution.py:31
  7.6 12.9 %copy-start.14 = (f32[512]{0:T(512)S(1)}, f32[512]{0:T(512)}, u32[]{:S(2)}) copy-start(f32[512]{0:T(512)} %param.21) | copy-start | bytes 6148
  7.6 13.5 %copy-start.16 = (u32[32]{0:T(128)S(1)}, u32[32]{0:T(128)}, u32[]{:S(2)}) copy-start(u32[32]{0:T(128)} %constant.72) | copy-start | bytes 388
  7.6 14.7 %copy-start.12 = (f32[1,2]{1,0:T(1,128)S(1)}, f32[1,2]{1,0:T(1,128)}, u32[]{:S(2)}) copy-start(f32[1,2]{1,0:T(1,128)} %param.18) | copy-start | bytes 28
  7.6 15.3 %copy-start.5 = (f32[16,1,2,1024]{3,2,1,0:T(2,128)S(1)}, f32[16,1,2,1024]{3,2,1,0:T(2,128)}, u32[]{:S(2)}) copy-start(f32[16,1,2,1024]{3,2,1,0:T(2,128)} %param.13) | copy-start | bytes 393220
  8.6 137.1 %all-to-all-start = ((f32[2,2,1,2,49,256]{5,1,4,3,2,0:T(2,128)}), f32[2,2,1,2,49,256]{5,1,4,3,2,0:T(2,128)}, u32[]{:S(2)}, u32[]{:S(2)}) async-start(f32[2,2,1,2,49,256]{5,1,4,3,2,0:T(2,128)} %pad_maximum_fusion), calls=%async_computation | async-start | bytes 802816 | tf_op jit(solution)/shard_map/all_to_all | solution.py:16
  23.8 100.3 %copy-start.1 = (f32[16,1,2,32,32]{4,3,0,2,1:T(8,128)S(1)}, f32[16,1,2,32,32]{4,3,0,2,1:T(8,128)}, u32[]{:S(2)}) copy-start(f32[16,1,2,32,32]{4,3,0,2,1:T(8,128)} %reshape.284) | copy-start | bytes 393220
  50.6 1.2 copy-start.2
  50.6 1.4 copy-start.3
  87.4 1.2 copy-start.2
  87.4 1.4 copy-start.3
  130.5 4.1 %copy-start.6 = (f32[16,1,2,1024]{3,2,1,0:T(2,128)S(1)}, f32[16,1,2,1024]{3,2,1,0:T(2,128)}, u32[]{:S(2)}) copy-start(f32[16,1,2,1024]{3,2,1,0:T(2,128)} %param.13) | copy-start | bytes 393220
  131.9 15.0 %copy-start.10 = (f32[16,2]{0,1:T(2,128)S(1)}, f32[16,2]{0,1:T(2,128)}, u32[]{:S(2)}) copy-start(f32[16,2]{0,1:T(2,128)} %get-tuple-element.87) | copy-start | bytes 388
  133.6 15.1 %copy-start.11 = (f32[256]{0:T(256)S(1)}, f32[256]{0:T(256)}, u32[]{:S(2)}) copy-start(f32[256]{0:T(256)} %dynamic_slice.14) | copy-start | bytes 3076
  133.6 20.2 %copy-start.13 = (f32[16]{0:T(128)S(1)}, f32[16]{0:T(128)}, u32[]{:S(2)}) copy-start(f32[16]{0:T(128)} %get-tuple-element.86) | copy-start | bytes 196
  133.6 49.7 %copy-start.9 = (f32[16,256]{1,0:T(8,128)S(1)}, f32[16,256]{1,0:T(8,128)}, u32[]{:S(2)}) copy-start(f32[16,256]{1,0:T(8,128)} %param.22) | copy-start | bytes 49156
  133.6 49.8 %copy-start.15 = (pred[49]{0:T(512)(128)(4,1)S(1)}, pred[49]{0:T(512)(128)(4,1)}, u32[]{:S(2)}) copy-start(pred[49]{0:T(512)(128)(4,1)} %iota_compare_fusion) | copy-start | bytes 151
  133.6 49.9 %copy-start.8 = (f32[16,49,256]{2,0,1:T(8,128)S(1)}, f32[16,49,256]{2,0,1:T(8,128)}, u32[]{:S(2)}) copy-start(f32[16,49,256]{2,0,1:T(8,128)} %param.23) | copy-start | bytes 2408452
  148.7 35.9 %copy-start.4 = (f32[16,49,256]{2,0,1:T(8,128)}, f32[16,49,256]{2,0,1:T(8,128)S(1)}, u32[]{:S(2)}) copy-start(f32[16,49,256]{2,0,1:T(8,128)S(1)} %fusion.19) | copy-start | bytes 2408452
